TPU v7x, 512 devices: a whole 4x4x16 slice. The times are simulated.
512 devices in a mesh: mode: 16 (over z_lo, y), cell: 32 (over z_hi, x, core).
Axes of the slice: x: 4, y: 4, z: 16 (z_hi: 4, z_lo: 4; z = z_hi * 4 + z_lo), core: 2. Of those that a mesh axis runs over, the one named last changes fastest.
Arguments:
- populations: float32 [2048, 1, 64, 128], P('mode', None, 'cell'), may hold values from -6 to 6
- contact_mask: int32 [1, 64, 128], P(None, 'cell'), may hold values 0 or 1
- octant: int32 [2048], P('mode'), may hold values from 0 to 7
- courant: float32 [3, 2048], P(None, 'mode'), may hold values from 0.03 to 0.3
- collision: bfloat16 [2048, 2048], P('mode'), as said below
Outputs:
- advanced: float32 [2048, 1, 64, 128], P('mode', None, 'cell')
Inputs may be any that keep to these rules, and one draw needn't show every extreme that they name: `collision`: diagonal entries between 0.1 and 0.6, off-diagonal ones small, all independent.
All inputs are finite; a program needn't handle non-finite values. No bound on the sum of `contact_mask` on one device may be relied on, other than what follows from the above.
Results may differ from a plain program's by a relative error of at most 0.0014.
Values may be sent and summed in bfloat16 or wider, within the bound.
A program may use at most 64 MiB of HBM per device.

v0:
```python
import jax
import jax.numpy as jnp
from jax import lax
from jax.sharding import PartitionSpec as P


def with_halo(block, sides, width):
    for axis, dim in sides:
        count = lax.axis_size(axis)
        forward = [(i, i + 1) for i in range(count - 1)]
        backward = [(target, source) for source, target in forward]
        low = lax.ppermute(
            lax.slice_in_dim(block, block.shape[dim] - width, None, axis=dim), axis, forward
        )
        high = lax.ppermute(lax.slice_in_dim(block, 0, width, axis=dim), axis, backward)
        block = jnp.concatenate([low, block, high], axis=dim)
    return block


def velocities(octant, courant):
    bits = [octant % 2, octant // 2 % 2, octant // 4 % 2]
    return [(1.0 - 2.0 * bits[d].astype(jnp.float32)) * courant[d] for d in range(3)]


def advect(field, speeds):
    vx, vy, vz = [s[:, None, None, None] for s in speeds]
    back_x = jnp.roll(field, 1, axis=3)
    ahead_x = jnp.roll(field, -1, axis=3)
    padded_y = with_halo(field.astype(jnp.bfloat16), (("cell", 2),), 1).astype(field.dtype)
    padded_z = jnp.pad(field, ((0, 0), (1, 1), (0, 0), (0, 0)))
    total = jnp.maximum(vx, 0.0) * (field - back_x) + jnp.minimum(vx, 0.0) * (ahead_x - field)
    total = (
        total
        + jnp.maximum(vy, 0.0) * (field - padded_y[:, :, :-2])
        + jnp.minimum(vy, 0.0) * (padded_y[:, :, 2:] - field)
    )
    total = (
        total
        + jnp.maximum(vz, 0.0) * (field - padded_z[:, :-2])
        + jnp.minimum(vz, 0.0) * (padded_z[:, 2:] - field)
    )
    return total


def collide(field, collision):
    rounded = field.astype(jnp.bfloat16).reshape(field.shape[0], -1)
    result = jnp.dot(
        collision,
        lax.all_gather(rounded, "mode", axis=0, tiled=True),
        preferred_element_type=jnp.float32,
    )
    return result.reshape(field.shape)


def on_device(populations, contact_mask, octant, courant, collision):
    keep = (1 - contact_mask).astype(jnp.float32)[None]
    speeds = velocities(octant, courant)
    first = keep * populations
    second = keep * (first - advect(first, speeds) - collide(first, collision))
    final = second - advect(second, speeds) - collide(second, collision)
    return keep * (0.5 * first + 0.5 * final)


def solution(mesh):
    placed = (
        P("mode", None, "cell", None),
        P(None, "cell", None),
        P("mode"),
        P(None, "mode"),
        P("mode", None),
    )
    return jax.shard_map(
        on_device,
        mesh=mesh,
        in_specs=placed,
        out_specs=P("mode", None, "cell", None),
        check_vma=False,
    )
```

profile of v0, /device:TPU:2, one launch (start us, length us, event | category | flops | bytes accessed | tf_op | source)
XLA Modules:
  0.0 199.0 jit_solution(11834423455826668827)
XLA Ops:
  6.5 0.0 copy-start
  6.5 0.0 all-gather.3.cloned.1.call-start
  6.5 0.7 convert_bitcast_fusion
  7.3 1.0 fusion.38
  8.3 0.6 copy.13
  8.9 0.0 all-gather.3.cloned.1.call-update
  8.9 0.0 all-gather.5.cloned.1.call-start
  9.0 0.1 fusion.44
  9.1 0.0 copy-start.2
  9.1 0.0 copy-start.3
  9.1 1.9 collective-permute-start.1
  11.0 2.4 %collective-permute-start = (bf16[128,1,1,128]{3,2,1,0:T(2,128)(2,1)S(1)}, bf16[128,1,1,128]{3,2,1,0:T(2,128)(2,1)S(1)}, u32[]{:S(2)}, u32[]{:S(2)}) collective-permute-start(bf16[128,1,1,128]{3,2,1,0:T(2,128)(2,1)S(1)} %get-tuple-element.25), channel_id=1, source_target_pairs={{0,1},{1,2},{2,3},{3,4},{4,5},{5,6},{6,7},{7,8},{8,9},{9,10},{10,1... | collective-permute-start | bytes 98312 | tf_op jit(solution)/shard_map/ppermute | solution.py:12
  13.4 0.0 copy-done.2
  13.5 0.0 copy-done.3
  13.5 0.2 fusion.41
  13.7 0.2 fusion.42
  13.9 0.0 collective-permute-done.1
  13.9 6.9 %collective-permute-done = bf16[128,1,1,128]{3,2,1,0:T(2,128)(2,1)S(1)} collective-permute-done((bf16[128,1,1,128]{3,2,1,0:T(2,128)(2,1)S(1)}, bf16[128,1,1,128]{3,2,1,0:T(2,128)(2,1)S(1)}, u32[]{:S(2)}, u32[]{:S(2)}) %collective-permute-start) | collective-permute-done | bytes 32800 | tf_op jit(solution)/shard_map/ppermute | solution.py:12
  20.9 0.2 maximum_convert_fusion
  21.1 78.8 %all-gather.3.cloned.1.call-done = bf16[2048,256]{1,0:T(8,128)(2,1)} async-done(((bf16[128,256]{1,0:T(8,128)(2,1)}), bf16[2048,256]{1,0:T(8,128)(2,1)}) %all-gather.3.cloned.1.call-update) | async-done | bytes 1048592 | tf_op jit(solution)/shard_map/all_gather | solution.py:49
  99.9 0.0 copy-done
  99.9 1.7 fusion.45
  101.6 0.1 copy.6
  101.7 1.4 fusion.34
  103.1 0.6 copy.12
  103.7 0.0 copy-start.1
  103.7 0.0 all-gather.5.cloned.1.call-update
  103.8 0.7 copy-done.1
  104.4 0.1 fusion.43
  104.5 1.9 collective-permute-start.3
  106.4 2.4 %collective-permute-start.2 = (bf16[128,1,1,128]{3,2,1,0:T(2,128)(2,1)S(1)}, bf16[128,1,1,128]{3,2,1,0:T(2,128)(2,1)S(1)}, u32[]{:S(2)}, u32[]{:S(2)}) collective-permute-start(bf16[128,1,1,128]{3,2,1,0:T(2,128)(2,1)S(1)} %get-tuple-element.23), channel_id=1, source_target_pairs={{0,1},{1,2},{2,3},{3,4},{4,5},{5,6},{6,7},{7,8},{8,9},{9,10},{10,1... | collective-permute-start | bytes 98312 | tf_op jit(solution)/shard_map/ppermute | solution.py:12
  108.9 0.2 fusion.39
  109.1 0.2 fusion.40
  109.3 0.0 collective-permute-done.3
  109.3 2.8 %collective-permute-done.2 = bf16[128,1,1,128]{3,2,1,0:T(2,128)(2,1)S(1)} collective-permute-done((bf16[128,1,1,128]{3,2,1,0:T(2,128)(2,1)S(1)}, bf16[128,1,1,128]{3,2,1,0:T(2,128)(2,1)S(1)}, u32[]{:S(2)}, u32[]{:S(2)}) %collective-permute-start.2) | collective-permute-done | bytes 32800 | tf_op jit(solution)/shard_map/ppermute | solution.py:12
  112.0 0.2 maximum_convert_fusion.1
  112.2 76.0 %all-gather.5.cloned.1.call-done = bf16[2048,256]{1,0:T(8,128)(2,1)} async-done(((bf16[128,256]{1,0:T(8,128)(2,1)}), bf16[2048,256]{1,0:T(8,128)(2,1)}) %all-gather.5.cloned.1.call-update) | async-done | bytes 1048592 | tf_op jit(solution)/shard_map/all_gather | solution.py:49
  188.2 1.7 fusion.46
  189.9 0.1 copy.7
  190.1 2.2 %add_multiply_fusion = f32[128,1,2,128]{3,2,1,0:T(2,128)} fusion(f32[128,1,2,128]{3,2,1,0:T(2,128)S(1)} %get-tuple-element.14, f32[128,1,2,128]{3,2,1,0:T(2,128)S(1)} %copy.7, f32[128,1,2,128]{3,2,1,0:T(2,128)S(1)} %get-tuple-element.6, f32[128,1,4,128]{3,2,1,0:T(4,128)S(1)} %maximum_convert_fusion.1, f32[128,1,2,1]{3,2,1,0:T(2,128)S(1)} %get-tuple-element.16, ...), kind=kLoop, calls=%fused_computation.30 | loop fusion | flops 720896 | bytes 1052672 | tf_op jit(solution)/shard_map/mul | solution.py:61
  (4 shorter events, 0.0 us)
Async XLA Ops:
  6.5 93.3 %copy-start = (bf16[128,2048]{1,0:T(8,128)(2,1)S(1)}, bf16[128,2048]{1,0:T(8,128)(2,1)}, u32[]{:S(2)}) copy-start(bf16[128,2048]{1,0:T(8,128)(2,1)} %param.9) | copy-start | bytes 1572868
  6.5 93.3 %all-gather.3.cloned.1.call-start = ((), (), s32[]{:S(2)}) async-start(), calls=%async_computation | async-start | bytes 1114112 | tf_op jit(solution)/shard_map/all_gather | solution.py:49
  8.9 179.3 %all-gather.5.cloned.1.call-start = ((), (), s32[]{:S(2)}) async-start(), calls=%async_computation.1 | async-start | bytes 1114112 | tf_op jit(solution)/shard_map/all_gather | solution.py:49
  9.1 4.4 %copy-start.2 = (f32[3,128]{1,0:T(4,128)S(1)}, f32[3,128]{1,0:T(4,128)}, u32[]{:S(2)}) copy-start(f32[3,128]{1,0:T(4,128)} %param.8) | copy-start | bytes 4612
  9.1 4.4 %copy-start.3 = (s32[128]{0:T(128)S(1)}, s32[128]{0:T(128)}, u32[]{:S(2)}) copy-start(s32[128]{0:T(128)} %param.7) | copy-start | bytes 1540
  9.1 4.8 %collective-permute-start.1 = (bf16[128,1,1,128]{3,2,1,0:T(2,128)(2,1)S(1)}, bf16[128,1,1,128]{3,2,1,0:T(2,128)(2,1)S(1)}, u32[]{:S(2)}, u32[]{:S(2)}) collective-permute-start(bf16[128,1,1,128]{3,2,1,0:T(2,128)(2,1)S(1)} %get-tuple-element.26), channel_id=1, source_target_pairs={{1,0},{2,1},{3,2},{4,3},{5,4},{6,5},{7,6},{8,7},{9,8},{10,9},{11,1... | collective-permute-start | bytes 98312 | tf_op jit(solution)/shard_map/ppermute | solution.py:15
  11.0 9.8 %collective-permute-start = (bf16[128,1,1,128]{3,2,1,0:T(2,128)(2,1)S(1)}, bf16[128,1,1,128]{3,2,1,0:T(2,128)(2,1)S(1)}, u32[]{:S(2)}, u32[]{:S(2)}) collective-permute-start(bf16[128,1,1,128]{3,2,1,0:T(2,128)(2,1)S(1)} %get-tuple-element.25), channel_id=1, source_target_pairs={{0,1},{1,2},{2,3},{3,4},{4,5},{5,6},{6,7},{7,8},{8,9},{9,10},{10,1... | collective-permute-start | bytes 98312 | tf_op jit(solution)/shard_map/ppermute | solution.py:12
  103.7 0.7 copy-start.1
  104.5 4.8 %collective-permute-start.3 = (bf16[128,1,1,128]{3,2,1,0:T(2,128)(2,1)S(1)}, bf16[128,1,1,128]{3,2,1,0:T(2,128)(2,1)S(1)}, u32[]{:S(2)}, u32[]{:S(2)}) collective-permute-start(bf16[128,1,1,128]{3,2,1,0:T(2,128)(2,1)S(1)} %get-tuple-element.24), channel_id=1, source_target_pairs={{1,0},{2,1},{3,2},{4,3},{5,4},{6,5},{7,6},{8,7},{9,8},{10,9},{11,1... | collective-permute-start | bytes 98312 | tf_op jit(solution)/shard_map/ppermute | solution.py:15
  106.4 5.6 %collective-permute-start.2 = (bf16[128,1,1,128]{3,2,1,0:T(2,128)(2,1)S(1)}, bf16[128,1,1,128]{3,2,1,0:T(2,128)(2,1)S(1)}, u32[]{:S(2)}, u32[]{:S(2)}) collective-permute-start(bf16[128,1,1,128]{3,2,1,0:T(2,128)(2,1)S(1)} %get-tuple-element.23), channel_id=1, source_target_pairs={{0,1},{1,2},{2,3},{3,4},{4,5},{5,6},{6,7},{7,8},{8,9},{9,10},{10,1... | collective-permute-start | bytes 98312 | tf_op jit(solution)/shard_map/ppermute | solution.py:12
Sparse Core Ops, SparseCore 0:
  9.4 90.4 all-gather.2
  103.9 84.3 all-gather.4
where the time goes:
time: 199 us
  waiting for transfers between devices  165 us (83%)
  between operations  13.5 us (7%)
  starting transfers between devices  8.7 us (4%)
  other arithmetic  5.72 us (3%)
  matrix products  3.38 us (2%)
  local copies, waits for them, and re-layouts  3.18 us (2%)
    all_gather x2, waiting for transfers between devices, collide(): lax.all_gather(rounded, 'mode', axis=0, tiled=True)  155 us
    ppermute x2, waiting for transfers between devices, with_halo(): lax.ppermute(lax.slice_in_dim(block, block.shape[dim] - width, None, axis...  9.69 us
    ppermute x2, starting transfers between devices, with_halo(): lax.ppermute(lax.slice_in_dim(block, block.shape[dim] - width, None, axis...  4.81 us
  transfers between devices with their start and end apart: 6, of which 4 were waited for; matrix products, arithmetic and copies ran while one was open for 1% of the time, Pallas kernels for 0%

commit v1 on v0

v1 whole, which is shorter than its diff:
```python
import jax
import jax.numpy as jnp
from jax import lax
from jax.experimental import pallas as pl
from jax.experimental.pallas import tpu as pltpu
from jax.sharding import PartitionSpec as P


B = 128
MESH = pl.DeviceIdType.MESH
F32, BF16 = jnp.float32, jnp.bfloat16


def kernel(
    pop_hbm, mask_hbm, octant_hbm, courant_hbm, coll_hbm, out_ref,
    pop, mask, octant, courant, speed, blocks, gathered, halo, sums, outgoing, incoming, field,
    load_sem, block_sem, blocks_send, blocks_recv, gather_send, gather_recv, halo_send, halo_recv, part_send, part_recv,
):
    mode, cell = lax.axis_index("mode"), lax.axis_index("cell")
    y, zl = mode % 4, mode // 4
    core, x, zh = cell % 2, cell // 2 % 4, cell // 8
    g = (1 - core) * y + core * zl
    s = (1 - core) * zl + core * y

    def on_gather_axis(place):
        return (1 - core) * (zl * 4 + place) + core * (place * 4 + y)

    def on_scatter_axis(place):
        return (1 - core) * (place * 4 + y) + core * (zl * 4 + place)

    def shifted_z(shift):
        z = (zh * 4 + zl + shift + 16) % 16
        return z % 4 * 4 + y, (z // 4 * 4 + x) * 2 + core

    def block_target(d):
        shift = (1, 2 - 4 * (zl % 2), -1)[d - 1]
        there_mode, there_cell = shifted_z(shift)
        return (
            (1 - core) * there_mode + core * on_scatter_axis((s + d) % 4),
            (1 - core) * there_cell + core * cell,
        )

    barrier = pltpu.get_barrier_semaphore()

    def greet(m, c):
        pl.semaphore_signal(barrier, 1, device_id=(m, c), device_id_type=MESH)

    for d in (1, 2, 3):
        greet(on_gather_axis((g + d) % 4), cell)
        greet(on_scatter_axis((s + d) % 4), cell)

    @pl.when(core == 0)
    def _():
        for shift in (1, -1, 2, -2):
            greet(*shifted_z(shift))

    @pl.when(cell > 0)
    def _():
        greet(mode, cell - 1)

    @pl.when(cell < 31)
    def _():
        greet(mode, cell + 1)

    loads = [
        pltpu.make_async_copy(pop_hbm, pop, load_sem.at[0]),
        pltpu.make_async_copy(mask_hbm, mask, load_sem.at[1]),
        pltpu.make_async_copy(octant_hbm, octant, load_sem.at[2]),
        pltpu.make_async_copy(courant_hbm, courant, load_sem.at[3]),
    ]
    for load in loads:
        load.start()

    def columns(place, i):
        return pl.ds(pl.multiple_of(((1 - core) * (place * 4 + i) + core * (i * 4 + place)) * B, B), B)

    own_blocks = [
        pltpu.make_async_copy(
            coll_hbm.at[:, columns(s, i)], blocks.at[s, :, pl.ds(i * B, B)], block_sem.at[i]
        )
        for i in range(4)
    ]
    for copy in own_blocks:
        copy.start()

    loads[0].wait()
    loads[1].wait()
    keep = (1 - mask[...]).astype(F32)
    keeps = [keep[r : r + 1, :] for r in (0, 1)]
    rows = pl.ds(pl.multiple_of(g * B, B), B)
    for r in (0, 1):
        first = keeps[r] * pop[pl.ds(r, B, stride=2), :]
        field[0, r] = first
        gathered[0, r, rows, :] = first.astype(BF16)

    @pl.when(cell == 0)
    def _():
        for stage in (0, 1):
            halo[stage, 0] = jnp.zeros((B, B), BF16)

    @pl.when(cell == 31)
    def _():
        for stage in (0, 1):
            halo[stage, 1] = jnp.zeros((B, B), BF16)

    pl.semaphore_wait(
        barrier,
        6 + 4 * (1 - core) + jnp.where(cell > 0, 1, 0) + jnp.where(cell < 31, 1, 0),
    )

    def gather_copy(stage, r, d):
        mine = gathered.at[stage, r, rows, :]
        return pltpu.make_async_remote_copy(
            mine, mine, gather_send.at[stage, r, d - 1], gather_recv.at[stage, r, d - 1],
            device_id=(on_gather_axis((g + d) % 4), cell), device_id_type=MESH,
        )

    def halo_copy(stage, side):
        return pltpu.make_async_remote_copy(
            gathered.at[stage, 1 - side, rows, :], halo.at[stage, side],
            halo_send.at[stage, side], halo_recv.at[stage, side],
            device_id=(mode, jnp.where(side == 0, jnp.minimum(cell + 1, 31), jnp.maximum(cell - 1, 0))), device_id_type=MESH,
        )

    def block_copies(d):
        m, c = block_target(d)
        return [
            pltpu.make_async_remote_copy(
                coll_hbm.at[:, columns((s + d) % 4, i)], blocks.at[s, :, pl.ds(i * B, B)],
                blocks_send.at[d - 1, i], blocks_recv.at[d - 1, i],
                device_id=(m, c), device_id_type=MESH,
            )
            for i in range(4)
        ]

    def part_copy(stage, r, d):
        return pltpu.make_async_remote_copy(
            outgoing.at[stage, r, d - 1], incoming.at[stage, r, d - 1],
            part_send.at[stage, r, d - 1], part_recv.at[stage, r, d - 1],
            device_id=(on_scatter_axis((s + d) % 4), cell), device_id_type=MESH,
        )

    def send_halo(stage):
        @pl.when(cell < 31)
        def _():
            halo_copy(stage, 0).start()

        @pl.when(cell > 0)
        def _():
            halo_copy(stage, 1).start()

    def wait_halo(stage):
        @pl.when(cell > 0)
        def _():
            halo_copy(stage, 0).wait_recv()

        @pl.when(cell < 31)
        def _():
            halo_copy(stage, 1).wait_recv()

    for r in (0, 1):
        for d in (2, 1, 3):
            gather_copy(0, r, d).start()
    for d in (2, 1, 3):
        for copy in block_copies(d):
            copy.start()
    send_halo(0)

    loads[2].wait()
    loads[3].wait()
    signs = octant[...]
    total = None
    for axis in range(3):
        bit = (signs // (2**axis)) % 2
        v = (1.0 - 2.0 * bit.astype(F32)) * courant[axis : axis + 1, :]
        v = jnp.transpose(jnp.broadcast_to(v, (B, B)))
        up, down = jnp.maximum(v, 0.0), jnp.minimum(v, 0.0)
        if axis < 2:
            speed[2 * axis] = up
            speed[2 * axis + 1] = down
        total = up - down if total is None else total + (up - down)
    speed[4] = total

    def advected(stage, r):
        f = field[stage, r]
        low = field[stage, 0] if r == 1 else halo[stage, 0].astype(F32)
        high = field[stage, 1] if r == 0 else halo[stage, 1].astype(F32)
        adv = speed[4] * f - speed[0] * pltpu.roll(f, 1, 1) + speed[1] * pltpu.roll(f, B - 1, 1)
        return f - (adv - speed[2] * low + speed[3] * high)

    for stage in (0, 1):
        if stage == 0:
            for copy in own_blocks:
                copy.wait()
        for r in (0, 1):
            for d in (1, 2, 3):
                gather_copy(stage, r, d).wait_recv()
            q = gathered[stage, r]
            for d in (2, 1, 3):
                if stage == 0 and r == 0:
                    for copy in block_copies(4 - d):
                        copy.wait_recv()
                part = jnp.dot(blocks[(s + d) % 4], q, preferred_element_type=F32)
                outgoing[stage, r, d - 1] = part.astype(BF16)
                part_copy(stage, r, d).start()
            sums[r] = jnp.dot(blocks[s], q, preferred_element_type=F32)
        wait_halo(stage)
        for r in (0, 1):
            sums[r] = advected(stage, r) - sums[r]
        for r in (0, 1):
            for d in (1, 2, 3):
                part_copy(stage, r, d).wait_recv()
            rest = incoming[stage, r, 0].astype(F32) + incoming[stage, r, 1].astype(F32) + incoming[stage, r, 2].astype(F32)
            if stage == 0:
                second = keeps[r] * (sums[r] - rest)
                field[1, r] = second
                gathered[1, r, rows, :] = second.astype(BF16)
                for d in (2, 1, 3):
                    gather_copy(1, r, d).start()
            else:
                out_ref[pl.ds(r, B, stride=2), :] = keeps[r] * (0.5 * field[0, r] + 0.5 * (sums[r] - rest))
        if stage == 0:
            send_halo(1)

    for d in (1, 2, 3):
        for copy in block_copies(d):
            copy.wait_send()
    for stage in (0, 1):
        for r in (0, 1):
            for d in (1, 2, 3):
                gather_copy(stage, r, d).wait_send()
                part_copy(stage, r, d).wait_send()

        @pl.when(cell < 31)
        def _():
            halo_copy(stage, 0).wait_send()

        @pl.when(cell > 0)
        def _():
            halo_copy(stage, 1).wait_send()


def on_device(populations, contact_mask, octant, courant, collision):
    dma = pltpu.SemaphoreType.DMA
    out = pl.pallas_call(
        kernel,
        out_shape=jax.ShapeDtypeStruct((2 * B, B), F32),
        in_specs=[pl.BlockSpec(memory_space=pl.ANY)] * 5,
        out_specs=pl.BlockSpec(memory_space=pltpu.VMEM),
        scratch_shapes=[
            pltpu.VMEM((2 * B, B), F32),
            pltpu.VMEM((2, B), jnp.int32),
            pltpu.VMEM((1, B), jnp.int32),
            pltpu.VMEM((3, B), F32),
            pltpu.VMEM((5, B, B), F32),
            pltpu.VMEM((4, B, 4 * B), BF16),
            pltpu.VMEM((2, 2, 4 * B, B), BF16),
            pltpu.VMEM((2, 2, B, B), BF16),
            pltpu.VMEM((2, B, B), F32),
            pltpu.VMEM((2, 2, 3, B, B), BF16),
            pltpu.VMEM((2, 2, 3, B, B), BF16),
            pltpu.VMEM((2, 2, B, B), F32),
            dma((4,)),
            dma((4,)),
            dma((3, 4)),
            dma((3, 4)),
            dma((2, 2, 3)),
            dma((2, 2, 3)),
            dma((2, 2)),
            dma((2, 2)),
            dma((2, 2, 3)),
            dma((2, 2, 3)),
        ],
        compiler_params=pltpu.CompilerParams(collective_id=0, has_side_effects=True),
        name="heun",
    )(
        populations.reshape(2 * B, B),
        contact_mask.reshape(2, B),
        octant.reshape(1, B),
        courant,
        collision,
    )
    return out.reshape(populations.shape)


def solution(mesh):
    placed = (
        P("mode", None, "cell", None),
        P(None, "cell", None),
        P("mode"),
        P(None, "mode"),
        P("mode", None),
    )
    return jax.shard_map(
        on_device,
        mesh=mesh,
        in_specs=placed,
        out_specs=P("mode", None, "cell", None),
        check_vma=False,
    )
```

time: 199 us -> 37.8 us (0.19)
  the two profiles are of different devices: /device:TPU:2 before, /device:TPU:6 now
where the time goes in v1:
time: 37.8 us; the launch traced here: 37.7 us
  Pallas kernels  36.1 us (96%)
  local copies, waits for them, and re-layouts  1.57 us (4%)
    pallas_call x1, Pallas kernels, on_device(): pl.pallas_call(kernel, out_shape=jax.ShapeDtypeStruct((2 * B, B), F32), i...  36.1 us
    unnamed x1, local copies, waits for them, and re-layouts  1.57 us

profile of v1, /device:TPU:6, one launch (start us, length us, event | category | flops | bytes accessed | tf_op | source)
XLA Modules:
  0.0 37.7 jit_solution(55521655808381081)
XLA Ops:
  0.0 36.1 %heun.1 = f32[256,128]{1,0:T(8,128)} custom-call(f32[256,128]{1,0:T(8,128)} %bitcast.7, s32[2,128]{1,0:T(2,128)} %bitcast.8, s32[1,128]{1,0:T(1,128)} %bitcast.9, f32[3,128]{1,0:T(4,128)} %courant_hbm.1, bf16[128,2048]{1,0:T(8,128)(2,1)} %coll_hbm.1), custom_call_target="tpu_custom_call" | custom-call | tf_op jit(solution)/shard_map/heun/pallas_call | solution.py:245
  36.1 1.6 %copy.8 = f32[128,1,2,128]{3,2,1,0:T(2,128)} copy(f32[128,1,2,128]{3,2,1,0:T(2,128)} %bitcast.6) | data formatting | bytes 262144

commit v2 on v1

--- a/solution.py
+++ b/solution.py
@@ -14,11 +14,12 @@
 def kernel(
     pop_hbm, mask_hbm, octant_hbm, courant_hbm, coll_hbm, out_ref,
     pop, mask, octant, courant, speed, blocks, gathered, halo, sums, outgoing, incoming, field,
-    load_sem, block_sem, blocks_send, blocks_recv, gather_send, gather_recv, halo_send, halo_recv, part_send, part_recv,
+    load_sem, block_sem, blocks_send, blocks_recv, gather_send, gather_recv, halo_send, halo_recv, part_send, part_recv, far_sem, ready_sem,
 ):
     mode, cell = lax.axis_index("mode"), lax.axis_index("cell")
     y, zl = mode % 4, mode // 4
-    core, x, zh = cell % 2, cell // 2 % 4, cell // 8
+    hw_core, x, zh = cell % 2, cell // 2 % 4, cell // 8
+    core = 1 - hw_core
     g = (1 - core) * y + core * zl
     s = (1 - core) * zl + core * y
 
@@ -30,10 +31,10 @@
 
     def shifted_z(shift):
         z = (zh * 4 + zl + shift + 16) % 16
-        return z % 4 * 4 + y, (z // 4 * 4 + x) * 2 + core
+        return z % 4 * 4 + y, (z // 4 * 4 + x) * 2 + hw_core
 
     def block_target(d):
-        shift = (1, 2 - 4 * (zl % 2), -1)[d - 1]
+        shift = (1, 2 - 4 * (zl // 2), -1)[d - 1]
         there_mode, there_cell = shifted_z(shift)
         return (
             (1 - core) * there_mode + core * on_scatter_axis((s + d) % 4),
@@ -45,20 +46,31 @@
     def greet(m, c):
         pl.semaphore_signal(barrier, 1, device_id=(m, c), device_id_type=MESH)
 
+    late = ((cell % 8 == 7) & (zh == 2)) | ((cell % 8 == 0) & ((zh == 1) | (zh == 2)))
+    early = ((cell % 8 == 7) & (zh < 2)) | ((cell % 8 == 0) & (zh == 3))
+    ordered = late
+    partners = []
     for d in (1, 2, 3):
-        greet(on_gather_axis((g + d) % 4), cell)
-        greet(on_scatter_axis((s + d) % 4), cell)
+        for there in (on_gather_axis((g + d) % 4), on_scatter_axis((s + d) % 4)):
+            partners.append(there)
+
+            @pl.when(jnp.logical_not(ordered) | (there > mode))
+            def _(there=there):
+                greet(there, cell)
 
     @pl.when(core == 0)
     def _():
-        for shift in (1, -1, 2, -2):
+        for shift in (1, -1):
             greet(*shifted_z(shift))
 
-    @pl.when(cell > 0)
+    far_next = (cell % 8 == 7) & (cell < 31)
+    far_back = (cell % 8 == 0) & (cell > 0)
+
+    @pl.when((cell > 0) & jnp.logical_not(far_back & late))
     def _():
         greet(mode, cell - 1)
 
-    @pl.when(cell < 31)
+    @pl.when((cell < 31) & jnp.logical_not(far_next & late))
     def _():
         greet(mode, cell + 1)
 
@@ -105,8 +117,18 @@
 
     pl.semaphore_wait(
         barrier,
-        6 + 4 * (1 - core) + jnp.where(cell > 0, 1, 0) + jnp.where(cell < 31, 1, 0),
+        jnp.where(ordered, g + s, 6) + 2 * (1 - core) + jnp.where(cell > 0, 1, 0) + jnp.where(cell < 31, 1, 0) - jnp.where(early, 1, 0),
     )
+
+    @pl.when(late)
+    def _():
+        pl.semaphore_signal(far_sem, 1, device_id=(mode, jnp.where(far_next, cell + 1, cell - 1)), device_id_type=MESH)
+
+    for there in partners:
+
+        @pl.when(ordered & (there < mode))
+        def _(there=there):
+            pl.semaphore_signal(ready_sem, 1, device_id=(there, cell), device_id_type=MESH)
 
     def gather_copy(stage, r, d):
         mine = gathered.at[stage, r, rows, :]
@@ -141,11 +163,11 @@
         )
 
     def send_halo(stage):
-        @pl.when(cell < 31)
+        @pl.when((cell < 31) & (jnp.logical_not(far_next) if stage == 0 else True))
         def _():
             halo_copy(stage, 0).start()
 
-        @pl.when(cell > 0)
+        @pl.when((cell > 0) & (jnp.logical_not(far_back) if stage == 0 else True))
         def _():
             halo_copy(stage, 1).start()
 
@@ -158,13 +180,40 @@
         def _():
             halo_copy(stage, 1).wait_recv()
 
-    for r in (0, 1):
-        for d in (2, 1, 3):
-            gather_copy(0, r, d).start()
+    def send_far():
+        @pl.when(far_next)
+        def _():
+            halo_copy(0, 0).start()
+
+        @pl.when(far_back)
+        def _():
+            halo_copy(0, 1).start()
+
+    pl.when(late)(send_far)
+
+    for later in (False, True):
+        for r in (0, 1):
+            for d in (2, 1, 3):
+
+                @pl.when((jnp.logical_not(ordered) | (on_gather_axis((g + d) % 4) > mode)) == later)
+                def _(r=r, d=d):
+                    gather_copy(0, r, d).start()
+
+        if not later:
+
+            @pl.when(ordered & (g + s < 6))
+            def _():
+                pl.semaphore_wait(ready_sem, 6 - g - s)
+
     for d in (2, 1, 3):
         for copy in block_copies(d):
             copy.start()
     send_halo(0)
+
+    @pl.when(early)
+    def _():
+        pl.semaphore_wait(far_sem, 1)
+        send_far()
 
     loads[2].wait()
     loads[3].wait()
@@ -244,7 +293,7 @@
     dma = pltpu.SemaphoreType.DMA
     out = pl.pallas_call(
         kernel,
-        out_shape=jax.ShapeDtypeStruct((2 * B, B), F32),
+        out_shape=pltpu.VMEM((2 * B, B), F32),
         in_specs=[pl.BlockSpec(memory_space=pl.ANY)] * 5,
         out_specs=pl.BlockSpec(memory_space=pltpu.VMEM),
         scratch_shapes=[
@@ -270,6 +319,8 @@
             dma((2, 2)),
             dma((2, 2, 3)),
             dma((2, 2, 3)),
+            pltpu.SemaphoreType.REGULAR,
+            pltpu.SemaphoreType.REGULAR,
         ],
         compiler_params=pltpu.CompilerParams(collective_id=0, has_side_effects=True),
         name="heun",

time: 37.8 us -> 31 us (0.82)
  the two profiles are of different devices: /device:TPU:6 before, /device:TPU:129 now
where the time goes in v2:
time: 31 us; the launch traced here: 30.9 us
  Pallas kernels  30.2 us (97%)
  local copies, waits for them, and re-layouts  0.66 us (2%)
    pallas_call x1, Pallas kernels, on_device(): pl.pallas_call(kernel, out_shape=pltpu.VMEM((2 * B, B), F32), in_specs=[p...  30.2 us
    unnamed x1, local copies, waits for them, and re-layouts  0.66 us

profile of v2, /device:TPU:129, one launch (start us, length us, event | category | flops | bytes accessed | tf_op | source)
XLA Modules:
  0.0 30.9 jit_solution(3635492178882282266)
XLA Ops:
  0.0 30.2 %heun.1 = f32[256,128]{1,0:T(8,128)S(1)} custom-call(f32[256,128]{1,0:T(8,128)} %bitcast.7, s32[2,128]{1,0:T(2,128)} %bitcast.8, s32[1,128]{1,0:T(1,128)} %bitcast.9, f32[3,128]{1,0:T(4,128)} %courant_hbm.1, bf16[128,2048]{1,0:T(8,128)(2,1)} %coll_hbm.1), custom_call_target="tpu_custom_call" | custom-call | tf_op jit(solution)/shard_map/heun/pallas_call | solution.py:294
  30.2 0.7 %copy.8 = f32[128,1,2,128]{3,2,1,0:T(2,128)} copy(f32[128,1,2,128]{3,2,1,0:T(2,128)S(1)} %bitcast.6) | data formatting | bytes 262144

commit v3 on v2

--- a/solution.py
+++ b/solution.py
@@ -170,6 +170,11 @@
         @pl.when((cell > 0) & (jnp.logical_not(far_back) if stage == 0 else True))
         def _():
             halo_copy(stage, 1).start()
+
+    def send_halo_row(r):
+        @pl.when(cell < 31 if r else cell > 0)
+        def _():
+            halo_copy(1, 1 - r).start()
 
     def wait_halo(stage):
         @pl.when(cell > 0)
@@ -266,10 +271,9 @@
                 gathered[1, r, rows, :] = second.astype(BF16)
                 for d in (2, 1, 3):
                     gather_copy(1, r, d).start()
+                send_halo_row(r)
             else:
                 out_ref[pl.ds(r, B, stride=2), :] = keeps[r] * (0.5 * field[0, r] + 0.5 * (sums[r] - rest))
-        if stage == 0:
-            send_halo(1)
 
     for d in (1, 2, 3):
         for copy in block_copies(d):

time: 31 us -> 30.5 us (0.984)
  Pallas kernels: 30.2 us -> 29.8 us
    pallas_call x1, Pallas kernels: 30.2 us -> 29.8 us  [on_device(): pl.pallas_call(kernel, out_shape=pltpu.VMEM((2 * B, B), F32), in_specs=[p...]
where the time goes in v3:
time: 30.5 us; the launch traced here: 30.4 us
  Pallas kernels  29.8 us (98%)
  local copies, waits for them, and re-layouts  0.66 us (2%)
    pallas_call x1, Pallas kernels, on_device(): pl.pallas_call(kernel, out_shape=pltpu.VMEM((2 * B, B), F32), in_specs=[p...  29.8 us
    unnamed x1, local copies, waits for them, and re-layouts  0.66 us

profile of v3, /device:TPU:129, one launch (start us, length us, event | category | flops | bytes accessed | tf_op | source)
XLA Modules:
  0.0 30.4 jit_solution(3765650511578890311)
XLA Ops:
  0.0 29.8 %heun.1 = f32[256,128]{1,0:T(8,128)S(1)} custom-call(f32[256,128]{1,0:T(8,128)} %bitcast.7, s32[2,128]{1,0:T(2,128)} %bitcast.8, s32[1,128]{1,0:T(1,128)} %bitcast.9, f32[3,128]{1,0:T(4,128)} %courant_hbm.1, bf16[128,2048]{1,0:T(8,128)(2,1)} %coll_hbm.1), custom_call_target="tpu_custom_call" | custom-call | tf_op jit(solution)/shard_map/heun/pallas_call | solution.py:298
  29.8 0.7 %copy.8 = f32[128,1,2,128]{3,2,1,0:T(2,128)} copy(f32[128,1,2,128]{3,2,1,0:T(2,128)S(1)} %bitcast.6) | data formatting | bytes 262144

commit v4 on v3

--- a/solution.py
+++ b/solution.py
@@ -14,7 +14,7 @@
 def kernel(
     pop_hbm, mask_hbm, octant_hbm, courant_hbm, coll_hbm, out_ref,
     pop, mask, octant, courant, speed, blocks, gathered, halo, sums, outgoing, incoming, field,
-    load_sem, block_sem, blocks_send, blocks_recv, gather_send, gather_recv, halo_send, halo_recv, part_send, part_recv, far_sem, ready_sem,
+    load_sem, block_sem, blocks_send, blocks_recv, gather_send, gather_recv, halo_send, halo_recv, part_send, part_recv, far_sem,
 ):
     mode, cell = lax.axis_index("mode"), lax.axis_index("cell")
     y, zl = mode % 4, mode // 4
@@ -48,15 +48,9 @@
 
     late = ((cell % 8 == 7) & (zh == 2)) | ((cell % 8 == 0) & ((zh == 1) | (zh == 2)))
     early = ((cell % 8 == 7) & (zh < 2)) | ((cell % 8 == 0) & (zh == 3))
-    ordered = late
-    partners = []
     for d in (1, 2, 3):
-        for there in (on_gather_axis((g + d) % 4), on_scatter_axis((s + d) % 4)):
-            partners.append(there)
-
-            @pl.when(jnp.logical_not(ordered) | (there > mode))
-            def _(there=there):
-                greet(there, cell)
+        greet(on_gather_axis((g + d) % 4), cell)
+        greet(on_scatter_axis((s + d) % 4), cell)
 
     @pl.when(core == 0)
     def _():
@@ -117,18 +111,12 @@
 
     pl.semaphore_wait(
         barrier,
-        jnp.where(ordered, g + s, 6) + 2 * (1 - core) + jnp.where(cell > 0, 1, 0) + jnp.where(cell < 31, 1, 0) - jnp.where(early, 1, 0),
+        6 + 2 * (1 - core) + jnp.where(cell > 0, 1, 0) + jnp.where(cell < 31, 1, 0) - jnp.where(early, 1, 0),
     )
 
     @pl.when(late)
     def _():
         pl.semaphore_signal(far_sem, 1, device_id=(mode, jnp.where(far_next, cell + 1, cell - 1)), device_id_type=MESH)
-
-    for there in partners:
-
-        @pl.when(ordered & (there < mode))
-        def _(there=there):
-            pl.semaphore_signal(ready_sem, 1, device_id=(there, cell), device_id_type=MESH)
 
     def gather_copy(stage, r, d):
         mine = gathered.at[stage, r, rows, :]
@@ -196,24 +184,14 @@
 
     pl.when(late)(send_far)
 
-    for later in (False, True):
-        for r in (0, 1):
-            for d in (2, 1, 3):
-
-                @pl.when((jnp.logical_not(ordered) | (on_gather_axis((g + d) % 4) > mode)) == later)
-                def _(r=r, d=d):
-                    gather_copy(0, r, d).start()
-
-        if not later:
-
-            @pl.when(ordered & (g + s < 6))
-            def _():
-                pl.semaphore_wait(ready_sem, 6 - g - s)
-
+    for r in (0, 1):
+        for d in (2, 1, 3):
+            gather_copy(0, r, d).start()
+    send_halo(0)
     for d in (2, 1, 3):
         for copy in block_copies(d):
             copy.start()
-    send_halo(0)
+
 
     @pl.when(early)
     def _():
@@ -257,7 +235,8 @@
                 part = jnp.dot(blocks[(s + d) % 4], q, preferred_element_type=F32)
                 outgoing[stage, r, d - 1] = part.astype(BF16)
                 part_copy(stage, r, d).start()
-            sums[r] = jnp.dot(blocks[s], q, preferred_element_type=F32)
+        for r in (0, 1):
+            sums[r] = jnp.dot(blocks[s], gathered[stage, r], preferred_element_type=F32)
         wait_halo(stage)
         for r in (0, 1):
             sums[r] = advected(stage, r) - sums[r]
@@ -324,7 +303,6 @@
             dma((2, 2, 3)),
             dma((2, 2, 3)),
             pltpu.SemaphoreType.REGULAR,
-            pltpu.SemaphoreType.REGULAR,
         ],
         compiler_params=pltpu.CompilerParams(collective_id=0, has_side_effects=True),
         name="heun",

time: 30.5 us -> 30.4 us (level)
  the two profiles are of different devices: /device:TPU:129 before, /device:TPU:39 now
where the time goes in v4:
time: 30.4 us; the launch traced here: 30.3 us
  Pallas kernels  29.6 us (97%)
  local copies, waits for them, and re-layouts  0.66 us (2%)
    pallas_call x1, Pallas kernels, on_device(): pl.pallas_call(kernel, out_shape=pltpu.VMEM((2 * B, B), F32), in_specs=[p...  29.6 us
    unnamed x1, local copies, waits for them, and re-layouts  0.66 us

profile of v4, /device:TPU:39, one launch (start us, length us, event | category | flops | bytes accessed | tf_op | source)
XLA Modules:
  0.0 30.3 jit_solution(2899511771860291805)
XLA Ops:
  0.0 29.6 %heun.1 = f32[256,128]{1,0:T(8,128)S(1)} custom-call(f32[256,128]{1,0:T(8,128)} %bitcast.7, s32[2,128]{1,0:T(2,128)} %bitcast.8, s32[1,128]{1,0:T(1,128)} %bitcast.9, f32[3,128]{1,0:T(4,128)} %courant_hbm.1, bf16[128,2048]{1,0:T(8,128)(2,1)} %coll_hbm.1), custom_call_target="tpu_custom_call" | custom-call | tf_op jit(solution)/shard_map/heun/pallas_call | solution.py:277
  29.6 0.7 %copy.8 = f32[128,1,2,128]{3,2,1,0:T(2,128)} copy(f32[128,1,2,128]{3,2,1,0:T(2,128)S(1)} %bitcast.6) | data formatting | bytes 262144

commit v5 on v4

--- a/solution.py
+++ b/solution.py
@@ -41,6 +41,8 @@
             (1 - core) * there_cell + core * cell,
         )
 
+    flip = jnp.where(cell == 16, 1, 0)
+
     barrier = pltpu.get_barrier_semaphore()
 
     def greet(m, c):
@@ -164,14 +166,10 @@
         def _():
             halo_copy(1, 1 - r).start()
 
-    def wait_halo(stage):
-        @pl.when(cell > 0)
-        def _():
-            halo_copy(stage, 0).wait_recv()
-
-        @pl.when(cell < 31)
-        def _():
-            halo_copy(stage, 1).wait_recv()
+    def wait_halo(stage, side):
+        @pl.when(cell < 31 if side else cell > 0)
+        def _():
+            halo_copy(stage, side).wait_recv()
 
     def send_far():
         @pl.when(far_next)
@@ -184,9 +182,9 @@
 
     pl.when(late)(send_far)
 
-    for r in (0, 1):
+    for k in (0, 1):
         for d in (2, 1, 3):
-            gather_copy(0, r, d).start()
+            gather_copy(0, (k + flip) % 2, d).start()
     send_halo(0)
     for d in (2, 1, 3):
         for copy in block_copies(d):
@@ -224,12 +222,13 @@
         if stage == 0:
             for copy in own_blocks:
                 copy.wait()
-        for r in (0, 1):
+        for k in (0, 1):
+            r = (k + flip) % 2
             for d in (1, 2, 3):
                 gather_copy(stage, r, d).wait_recv()
             q = gathered[stage, r]
             for d in (2, 1, 3):
-                if stage == 0 and r == 0:
+                if stage == 0 and k == 0:
                     for copy in block_copies(4 - d):
                         copy.wait_recv()
                 part = jnp.dot(blocks[(s + d) % 4], q, preferred_element_type=F32)
@@ -237,22 +236,41 @@
                 part_copy(stage, r, d).start()
         for r in (0, 1):
             sums[r] = jnp.dot(blocks[s], gathered[stage, r], preferred_element_type=F32)
-        wait_halo(stage)
-        for r in (0, 1):
-            sums[r] = advected(stage, r) - sums[r]
-        for r in (0, 1):
+
+        def rest(stage, r):
             for d in (1, 2, 3):
                 part_copy(stage, r, d).wait_recv()
-            rest = incoming[stage, r, 0].astype(F32) + incoming[stage, r, 1].astype(F32) + incoming[stage, r, 2].astype(F32)
-            if stage == 0:
-                second = keeps[r] * (sums[r] - rest)
-                field[1, r] = second
-                gathered[1, r, rows, :] = second.astype(BF16)
-                for d in (2, 1, 3):
-                    gather_copy(1, r, d).start()
-                send_halo_row(r)
-            else:
-                out_ref[pl.ds(r, B, stride=2), :] = keeps[r] * (0.5 * field[0, r] + 0.5 * (sums[r] - rest))
+            return incoming[stage, r, 0].astype(F32) + incoming[stage, r, 1].astype(F32) + incoming[stage, r, 2].astype(F32)
+
+        def finish_first(r):
+            wait_halo(0, r)
+            base = advected(0, r) - sums[r]
+            second = keeps[r] * (base - rest(0, r))
+            field[1, r] = second
+            gathered[1, r, rows, :] = second.astype(BF16)
+            for d in (2, 1, 3):
+                gather_copy(1, r, d).start()
+            send_halo_row(r)
+
+        if stage == 0:
+
+            @pl.when(flip == 0)
+            def _():
+                finish_first(0)
+                finish_first(1)
+
+            @pl.when(flip == 1)
+            def _():
+                finish_first(1)
+                finish_first(0)
+
+        else:
+            for r in (0, 1):
+                wait_halo(1, r)
+            for r in (0, 1):
+                sums[r] = advected(1, r) - sums[r]
+            for r in (0, 1):
+                out_ref[pl.ds(r, B, stride=2), :] = keeps[r] * (0.5 * field[0, r] + 0.5 * (sums[r] - rest(1, r)))
 
     for d in (1, 2, 3):
         for copy in block_copies(d):

time: 30.4 us -> 30.4 us (level)
  no operation moved by 1% of the time
where the time goes in v5:
time: 30.4 us; the launch traced here: 30.3 us
  Pallas kernels  29.6 us (97%)
  local copies, waits for them, and re-layouts  0.66 us (2%)
    pallas_call x1, Pallas kernels, on_device(): pl.pallas_call(kernel, out_shape=pltpu.VMEM((2 * B, B), F32), in_specs=[p...  29.6 us
    unnamed x1, local copies, waits for them, and re-layouts  0.66 us

profile of v5, /device:TPU:39, one launch (start us, length us, event | category | flops | bytes accessed | tf_op | source)
XLA Modules:
  0.0 30.3 jit_solution(11152488854489731499)
XLA Ops:
  0.0 29.6 %heun.1 = f32[256,128]{1,0:T(8,128)S(1)} custom-call(f32[256,128]{1,0:T(8,128)} %bitcast.7, s32[2,128]{1,0:T(2,128)} %bitcast.8, s32[1,128]{1,0:T(1,128)} %bitcast.9, f32[3,128]{1,0:T(4,128)} %courant_hbm.1, bf16[128,2048]{1,0:T(8,128)(2,1)} %coll_hbm.1), custom_call_target="tpu_custom_call" | custom-call | tf_op jit(solution)/shard_map/heun/pallas_call | solution.py:295
  29.6 0.7 %copy.8 = f32[128,1,2,128]{3,2,1,0:T(2,128)} copy(f32[128,1,2,128]{3,2,1,0:T(2,128)S(1)} %bitcast.6) | data formatting | bytes 262144
